TPU v7x, 512 devices: a whole 4x8x8 slice. The times are simulated.
512 devices in a mesh: row: 8 (over y), col: 16 (over z, core), rep: 4 (over x).
Axes of the slice: x: 4, y: 8, z: 8, core: 2. Of those that a mesh axis runs over, the one named last changes fastest.
Arguments:
- p_values: float32 [256, 4, 12, 128, 128], P(('row', 'col'), 'rep'), may hold values from -2.5 to 2.5
- p_cols: int32 [1024, 12], replicated, may hold values from 0 to 1023, as said below
- out_cols: int32 [1024, 8], P(('row', 'col')), may hold values from 0 to 1023, as said below
Outputs:
- square: float32 [1024, 8, 128, 128], P(('row', 'col', 'rep'))
Inputs may be any that keep to these rules, and one draw needn't show every extreme that they name: `p_cols`: block row r names 12 distinct block columns c with r - 16 <= c < r + 16; its slots l * 3 to (l + 1) * 3 - 1 hold exactly the 3 columns that are congruent to l modulo 4. `out_cols`: block row r names 8 distinct block columns c with r - 16 <= c <= r + 16.
All inputs are finite; a program needn't handle non-finite values.
Results may differ from a plain program's by a relative error of at most 0.0003.
Values sent between devices are 32-bit elements; how exact they have to be, the bound alone decides.
No kernel may reach another device: no remote copies, remote signals or barrier semaphores. Data moves between devices by JAX's collectives and lax.ppermute only.
A program may use at most 64 MiB of HBM per device.

v0:
```python
import jax
import jax.numpy as jnp
from jax import lax
from jax.sharding import PartitionSpec as P

HIGHEST = lax.Precision.HIGHEST


def passed_along(x, axis, by):
    peers = lax.axis_size(axis)
    pairs = [(i, i + by) for i in range(peers) if 0 <= i + by < peers]
    return lax.ppermute(x, axis, pairs)


def on_device(p_values, p_cols, out_cols):
    layers = lax.axis_size("rep")
    layer_index = lax.axis_index("rep")
    segment = lax.axis_index(("row", "col"))
    own_rows = p_values[:, 0]
    row_count = own_rows.shape[0]
    slot_total = own_rows.shape[1]
    block_size = own_rows.shape[2]
    per_layer = slot_total // layers
    seg_rows = row_count * layers
    gathered = lax.all_gather(p_values, "rep", axis=1, tiled=True)
    entries = lax.dynamic_slice_in_dim(gathered, layer_index * per_layer, per_layer, 2)
    entries = entries.reshape(seg_rows, per_layer, block_size, block_size)
    received = []
    for offset in (2, 1, -1, -2):
        received.append(passed_along(own_rows, ("row", "col"), offset))
    window_rows = jnp.concatenate(
        [received[0], received[1], own_rows, received[2], received[3]], axis=0
    )
    inner_cols = lax.dynamic_slice(
        p_cols, (segment * seg_rows, layer_index * per_layer), (seg_rows, per_layer)
    )
    far_cols = p_cols[inner_cols]
    slot_ids = jnp.arange(slot_total, dtype=jnp.int32)
    matches = far_cols[:, :, None, :] == out_cols[:, None, :, None]
    slot_index = jnp.sum(jnp.where(matches, slot_ids, 0), axis=3)
    present = jnp.any(matches, axis=3)
    window_idx = inner_cols // layers - (segment - 2) * row_count

    def one_row(row_index):
        picked = window_rows[window_idx[row_index][:, None], slot_index[row_index]]
        picked = jnp.where(present[row_index][:, :, None, None], picked, jnp.zeros_like(picked))
        return jnp.einsum("sab,sfbc->fac", entries[row_index], picked, precision=HIGHEST)

    return lax.psum_scatter(
        lax.map(one_row, jnp.arange(row_count * lax.axis_size("rep"), dtype=jnp.int32)),
        "rep",
        scatter_dimension=0,
        tiled=True,
    )


def solution(mesh):
    in_specs = (P(("row", "col"), "rep", None, None, None), P(), P(("row", "col"), None))
    out_specs = P(("row", "col", "rep"), None, None, None)
    return jax.shard_map(
        on_device, mesh=mesh, in_specs=in_specs, out_specs=out_specs, check_vma=False
    )
```

profile of v0, /device:TPU:1, one launch (start us, length us, event | category | flops | bytes accessed | tf_op | source)
XLA Modules:
  0.0 234.3 jit_solution(4974504850985986855)
XLA Ops:
  7.3 6.0 %collective-permute-start = (f32[2,12,128,128]{3,2,1,0:T(8,128)}, f32[2,12,128,128]{3,2,1,0:T(8,128)}, u32[]{:S(2)}, u32[]{:S(2)}) collective-permute-start(f32[2,12,128,128]{3,2,1,0:T(8,128)} %bitcast.41), channel_id=1, source_target_pairs={{0,8},{4,12},{8,16},{12,20},{16,24},{20,28},{24,32},{28,36},{32,40... | collective-permute-start | bytes 4718600 | tf_op jit(solution)/shard_map/ppermute | solution.py:12
  13.3 3.7 %collective-permute-start.1 = (f32[2,12,128,128]{3,2,1,0:T(8,128)}, f32[2,12,128,128]{3,2,1,0:T(8,128)}, u32[]{:S(2)}, u32[]{:S(2)}) collective-permute-start(f32[2,12,128,128]{3,2,1,0:T(8,128)} %bitcast.42), channel_id=1, source_target_pairs={{0,4},{4,8},{8,12},{12,16},{16,20},{20,24},{24,28},{28,32},{32,36}... | collective-permute-start | bytes 4718600 | tf_op jit(solution)/shard_map/ppermute | solution.py:12
  17.0 4.0 %collective-permute-start.2 = (f32[2,12,128,128]{3,2,1,0:T(8,128)}, f32[2,12,128,128]{3,2,1,0:T(8,128)}, u32[]{:S(2)}, u32[]{:S(2)}) collective-permute-start(f32[2,12,128,128]{3,2,1,0:T(8,128)} %bitcast.43), channel_id=1, source_target_pairs={{4,0},{8,4},{12,8},{16,12},{20,16},{24,20},{28,24},{32,28},{36,32}... | collective-permute-start | bytes 4718600 | tf_op jit(solution)/shard_map/ppermute | solution.py:12
  21.0 1.3 collective-permute-start.3
  22.3 1.9 copy.17
  25.0 1.6 gather_fusion.1
  29.1 13.9 %collective-permute-done = f32[2,12,128,128]{3,2,1,0:T(8,128)} collective-permute-done((f32[2,12,128,128]{3,2,1,0:T(8,128)}, f32[2,12,128,128]{3,2,1,0:T(8,128)}, u32[]{:S(2)}, u32[]{:S(2)}) %collective-permute-start) | collective-permute-done | bytes 1572896 | tf_op jit(solution)/shard_map/ppermute | solution.py:12
  43.1 2.7 %constant_dynamic-update-slice_fusion.5 = f32[10,12,128,128]{3,2,1,0:T(8,128)} fusion(f32[2,12,128,128]{3,2,1,0:T(8,128)} %collective-permute-done), kind=kLoop, calls=%fused_computation.29 | loop fusion | bytes 3145728
  45.8 17.7 %collective-permute-done.1 = f32[2,12,128,128]{3,2,1,0:T(8,128)} collective-permute-done((f32[2,12,128,128]{3,2,1,0:T(8,128)}, f32[2,12,128,128]{3,2,1,0:T(8,128)}, u32[]{:S(2)}, u32[]{:S(2)}) %collective-permute-start.1) | collective-permute-done | bytes 1572896 | tf_op jit(solution)/shard_map/ppermute | solution.py:12
  63.5 2.7 %constant_dynamic-update-slice_fusion.4 = f32[10,12,128,128]{3,2,1,0:T(8,128)} fusion(f32[10,12,128,128]{3,2,1,0:T(8,128)} %constant_dynamic-update-slice_fusion.5, f32[2,12,128,128]{3,2,1,0:T(8,128)} %collective-permute-done.1), kind=kLoop, calls=%fused_computation.28 | loop fusion | bytes 3145728
  67.5 2.7 %constant_dynamic-update-slice_fusion.2 = f32[10,12,128,128]{3,2,1,0:T(8,128)} fusion(f32[10,12,128,128]{3,2,1,0:T(8,128)} %constant_dynamic-update-slice_fusion.3, f32[2,12,128,128]{3,2,1,0:T(8,128)} %collective-permute-done.2), kind=kLoop, calls=%fused_computation.26 | loop fusion | bytes 3145728
  70.2 1.3 constant_dynamic-update-slice_fusion.1
  71.5 14.5 %all-gather.2.cloned.1.call-done = f32[2,4,12,128,128]{4,3,2,1,0:T(8,128)} async-done(((f32[2,1,12,128,128]{4,3,2,1,0:T(8,128)}), f32[2,4,12,128,128]{4,3,2,1,0:T(8,128)}) %all-gather.2.cloned.1.call-update) | async-done | bytes 6291472 | tf_op jit(solution)/shard_map/all_gather | solution.py:25
  86.0 2.7 %constant_dynamic-slice_fusion.1 = f32[2,4,3,128,128]{4,3,2,1,0:T(8,128)} fusion(f32[2,4,12,128,128]{4,3,2,1,0:T(8,128)} %all-gather.2.cloned.1.call-done, s32[]{:T(128)S(6)} %select_n.48), kind=kLoop, calls=%fused_computation.40 | loop fusion | bytes 3145732 | tf_op jit(solution)/shard_map/dynamic_slice | solution.py:26
  88.7 85.6 %while.10 = (s32[]{:T(128)}, f32[8,8,128,128]{3,2,1,0:T(8,128)}, s32[8]{0:T(128)S(1)}, pred[8,3,8]{2,1,0:T(4,128)(4,1)S(1)}, s32[8,3]{1,0:T(8,128)S(1)}, /*index...) while((s32[]{:T(128)}, f32[8,8,128,128]{3,2,1,0:T(8,128)}, ...), condition=%wide.region_3.4_spmd, body=%wide.region_2.3_spmd.sunk | while | flops 604373184 | bytes 10683783 | solution.py:50
  91.4 3.9 %gather_fusion = f32[24,128,128]{2,1,0:T(8,128)S(1)} fusion(f32[10,12,128,128]{3,2,1,0:T(8,128)} %get-tuple-element.151, s32[24]{0:T(128)S(1)} %reshape.83), kind=kCustom, calls=%fused_computation.clone.1 | custom fusion | bytes 3145920 | tf_op jit(solution)/shard_map/while/body/eval_jaxpr/gather | solution.py:45
  95.9 2.4 %fusion.27 = f32[1,8,128,128]{2,3,1,0:T(8,128)S(1)} fusion(f32[3,8,128,128]{2,3,0,1:T(8,128)S(1)} %copy.26, pred[3,8]{0,1:T(8,128)(4,1)S(1)} %copy.27, f32[8,3,128,128]{3,2,1,0:T(8,128)} %get-tuple-element.152, s32[]{:T(128)S(6)} %select_n.82), kind=kOutput, calls=%fused_computation.4.clone.1 | convolution fusion | flops 604372992 | bytes 2293788 | tf_op jit(solution)/shard_map/while/body/eval_jaxpr/sab,sfbc->fac/dot_general | solution.py:47
  102.1 3.9 %gather_fusion = f32[24,128,128]{2,1,0:T(8,128)S(1)} fusion(f32[10,12,128,128]{3,2,1,0:T(8,128)} %get-tuple-element.151, s32[24]{0:T(128)S(1)} %reshape.83), kind=kCustom, calls=%fused_computation.clone.1 | custom fusion | bytes 3145920 | tf_op jit(solution)/shard_map/while/body/eval_jaxpr/gather | solution.py:45
  106.6 2.4 %fusion.27 = f32[1,8,128,128]{2,3,1,0:T(8,128)S(1)} fusion(f32[3,8,128,128]{2,3,0,1:T(8,128)S(1)} %copy.26, pred[3,8]{0,1:T(8,128)(4,1)S(1)} %copy.27, f32[8,3,128,128]{3,2,1,0:T(8,128)} %get-tuple-element.152, s32[]{:T(128)S(6)} %select_n.82), kind=kOutput, calls=%fused_computation.4.clone.1 | convolution fusion | flops 604372992 | bytes 2293788 | tf_op jit(solution)/shard_map/while/body/eval_jaxpr/sab,sfbc->fac/dot_general | solution.py:47
  112.8 3.9 %gather_fusion = f32[24,128,128]{2,1,0:T(8,128)S(1)} fusion(f32[10,12,128,128]{3,2,1,0:T(8,128)} %get-tuple-element.151, s32[24]{0:T(128)S(1)} %reshape.83), kind=kCustom, calls=%fused_computation.clone.1 | custom fusion | bytes 3145920 | tf_op jit(solution)/shard_map/while/body/eval_jaxpr/gather | solution.py:45
  117.3 2.4 %fusion.27 = f32[1,8,128,128]{2,3,1,0:T(8,128)S(1)} fusion(f32[3,8,128,128]{2,3,0,1:T(8,128)S(1)} %copy.26, pred[3,8]{0,1:T(8,128)(4,1)S(1)} %copy.27, f32[8,3,128,128]{3,2,1,0:T(8,128)} %get-tuple-element.152, s32[]{:T(128)S(6)} %select_n.82), kind=kOutput, calls=%fused_computation.4.clone.1 | convolution fusion | flops 604372992 | bytes 2293788 | tf_op jit(solution)/shard_map/while/body/eval_jaxpr/sab,sfbc->fac/dot_general | solution.py:47
  123.5 3.9 %gather_fusion = f32[24,128,128]{2,1,0:T(8,128)S(1)} fusion(f32[10,12,128,128]{3,2,1,0:T(8,128)} %get-tuple-element.151, s32[24]{0:T(128)S(1)} %reshape.83), kind=kCustom, calls=%fused_computation.clone.1 | custom fusion | bytes 3145920 | tf_op jit(solution)/shard_map/while/body/eval_jaxpr/gather | solution.py:45
  128.0 2.4 %fusion.27 = f32[1,8,128,128]{2,3,1,0:T(8,128)S(1)} fusion(f32[3,8,128,128]{2,3,0,1:T(8,128)S(1)} %copy.26, pred[3,8]{0,1:T(8,128)(4,1)S(1)} %copy.27, f32[8,3,128,128]{3,2,1,0:T(8,128)} %get-tuple-element.152, s32[]{:T(128)S(6)} %select_n.82), kind=kOutput, calls=%fused_computation.4.clone.1 | convolution fusion | flops 604372992 | bytes 2293788 | tf_op jit(solution)/shard_map/while/body/eval_jaxpr/sab,sfbc->fac/dot_general | solution.py:47
  134.2 3.9 %gather_fusion = f32[24,128,128]{2,1,0:T(8,128)S(1)} fusion(f32[10,12,128,128]{3,2,1,0:T(8,128)} %get-tuple-element.151, s32[24]{0:T(128)S(1)} %reshape.83), kind=kCustom, calls=%fused_computation.clone.1 | custom fusion | bytes 3145920 | tf_op jit(solution)/shard_map/while/body/eval_jaxpr/gather | solution.py:45
  138.7 2.4 %fusion.27 = f32[1,8,128,128]{2,3,1,0:T(8,128)S(1)} fusion(f32[3,8,128,128]{2,3,0,1:T(8,128)S(1)} %copy.26, pred[3,8]{0,1:T(8,128)(4,1)S(1)} %copy.27, f32[8,3,128,128]{3,2,1,0:T(8,128)} %get-tuple-element.152, s32[]{:T(128)S(6)} %select_n.82), kind=kOutput, calls=%fused_computation.4.clone.1 | convolution fusion | flops 604372992 | bytes 2293788 | tf_op jit(solution)/shard_map/while/body/eval_jaxpr/sab,sfbc->fac/dot_general | solution.py:47
  144.9 3.9 %gather_fusion = f32[24,128,128]{2,1,0:T(8,128)S(1)} fusion(f32[10,12,128,128]{3,2,1,0:T(8,128)} %get-tuple-element.151, s32[24]{0:T(128)S(1)} %reshape.83), kind=kCustom, calls=%fused_computation.clone.1 | custom fusion | bytes 3145920 | tf_op jit(solution)/shard_map/while/body/eval_jaxpr/gather | solution.py:45
  149.4 2.4 %fusion.27 = f32[1,8,128,128]{2,3,1,0:T(8,128)S(1)} fusion(f32[3,8,128,128]{2,3,0,1:T(8,128)S(1)} %copy.26, pred[3,8]{0,1:T(8,128)(4,1)S(1)} %copy.27, f32[8,3,128,128]{3,2,1,0:T(8,128)} %get-tuple-element.152, s32[]{:T(128)S(6)} %select_n.82), kind=kOutput, calls=%fused_computation.4.clone.1 | convolution fusion | flops 604372992 | bytes 2293788 | tf_op jit(solution)/shard_map/while/body/eval_jaxpr/sab,sfbc->fac/dot_general | solution.py:47
  155.6 3.9 %gather_fusion = f32[24,128,128]{2,1,0:T(8,128)S(1)} fusion(f32[10,12,128,128]{3,2,1,0:T(8,128)} %get-tuple-element.151, s32[24]{0:T(128)S(1)} %reshape.83), kind=kCustom, calls=%fused_computation.clone.1 | custom fusion | bytes 3145920 | tf_op jit(solution)/shard_map/while/body/eval_jaxpr/gather | solution.py:45
  160.1 2.4 %fusion.27 = f32[1,8,128,128]{2,3,1,0:T(8,128)S(1)} fusion(f32[3,8,128,128]{2,3,0,1:T(8,128)S(1)} %copy.26, pred[3,8]{0,1:T(8,128)(4,1)S(1)} %copy.27, f32[8,3,128,128]{3,2,1,0:T(8,128)} %get-tuple-element.152, s32[]{:T(128)S(6)} %select_n.82), kind=kOutput, calls=%fused_computation.4.clone.1 | convolution fusion | flops 604372992 | bytes 2293788 | tf_op jit(solution)/shard_map/while/body/eval_jaxpr/sab,sfbc->fac/dot_general | solution.py:47
  166.3 3.9 %gather_fusion = f32[24,128,128]{2,1,0:T(8,128)S(1)} fusion(f32[10,12,128,128]{3,2,1,0:T(8,128)} %get-tuple-element.151, s32[24]{0:T(128)S(1)} %reshape.83), kind=kCustom, calls=%fused_computation.clone.1 | custom fusion | bytes 3145920 | tf_op jit(solution)/shard_map/while/body/eval_jaxpr/gather | solution.py:45
  170.8 2.4 %fusion.27 = f32[1,8,128,128]{2,3,1,0:T(8,128)S(1)} fusion(f32[3,8,128,128]{2,3,0,1:T(8,128)S(1)} %copy.26, pred[3,8]{0,1:T(8,128)(4,1)S(1)} %copy.27, f32[8,3,128,128]{3,2,1,0:T(8,128)} %get-tuple-element.152, s32[]{:T(128)S(6)} %select_n.82), kind=kOutput, calls=%fused_computation.4.clone.1 | convolution fusion | flops 604372992 | bytes 2293788 | tf_op jit(solution)/shard_map/while/body/eval_jaxpr/sab,sfbc->fac/dot_general | solution.py:47
  174.3 53.1 %reduce-scatter.2.cloned.1.call-done = f32[2,8,128,128]{3,2,1,0:T(8,128)} async-done(((f32[8,8,128,128]{3,2,1,0:T(8,128)}), f32[2,8,128,128]{3,2,1,0:T(8,128)}) %reduce-scatter.2.cloned.1.call-update) | async-done | bytes 1048592 | tf_op jit(solution)/shard_map/reduce_scatter | solution.py:49
  (90 shorter events, 24.4 us)
Async XLA Ops:
  6.5 59.7 %copy-start = (f32[2,1,12,128,128]{4,3,2,1,0:T(8,128)S(1)}, f32[2,1,12,128,128]{4,3,2,1,0:T(8,128)}, u32[]{:S(2)}) copy-start(f32[2,1,12,128,128]{4,3,2,1,0:T(8,128)} %param.5) | copy-start | bytes 4718596
  6.5 79.4 %all-gather.2.cloned.1.call-start = ((), (), s32[]{:S(2)}) async-start(), calls=%async_computation.1 | async-start | bytes 7864320 | tf_op jit(solution)/shard_map/all_gather | solution.py:25
  7.3 220.2 %reduce-scatter.2.cloned.1.call-start = ((), (), s32[]{:S(2)}) async-start(), calls=%async_computation.2 | async-start | bytes 5242880 | tf_op jit(solution)/shard_map/reduce_scatter | solution.py:49
  7.3 35.8 %collective-permute-start = (f32[2,12,128,128]{3,2,1,0:T(8,128)}, f32[2,12,128,128]{3,2,1,0:T(8,128)}, u32[]{:S(2)}, u32[]{:S(2)}) collective-permute-start(f32[2,12,128,128]{3,2,1,0:T(8,128)} %bitcast.41), channel_id=1, source_target_pairs={{0,8},{4,12},{8,16},{12,20},{16,24},{20,28},{24,32},{28,36},{32,40... | collective-permute-start | bytes 4718600 | tf_op jit(solution)/shard_map/ppermute | solution.py:12
  13.3 50.2 %collective-permute-start.1 = (f32[2,12,128,128]{3,2,1,0:T(8,128)}, f32[2,12,128,128]{3,2,1,0:T(8,128)}, u32[]{:S(2)}, u32[]{:S(2)}) collective-permute-start(f32[2,12,128,128]{3,2,1,0:T(8,128)} %bitcast.42), channel_id=1, source_target_pairs={{0,4},{4,8},{8,12},{12,16},{16,20},{20,24},{24,28},{28,32},{32,36}... | collective-permute-start | bytes 4718600 | tf_op jit(solution)/shard_map/ppermute | solution.py:12
  17.0 50.5 %collective-permute-start.2 = (f32[2,12,128,128]{3,2,1,0:T(8,128)}, f32[2,12,128,128]{3,2,1,0:T(8,128)}, u32[]{:S(2)}, u32[]{:S(2)}) collective-permute-start(f32[2,12,128,128]{3,2,1,0:T(8,128)} %bitcast.43), channel_id=1, source_target_pairs={{4,0},{8,4},{12,8},{16,12},{20,16},{24,20},{28,24},{32,28},{36,32}... | collective-permute-start | bytes 4718600 | tf_op jit(solution)/shard_map/ppermute | solution.py:12
  21.0 49.2 %collective-permute-start.3 = (f32[2,12,128,128]{3,2,1,0:T(8,128)}, f32[2,12,128,128]{3,2,1,0:T(8,128)S(1)}, u32[]{:S(2)}, u32[]{:S(2)}) collective-permute-start(f32[2,12,128,128]{3,2,1,0:T(8,128)} %bitcast.44), channel_id=1, source_target_pairs={{8,0},{12,4},{16,8},{20,12},{24,16},{28,20},{32,24},{36,28},{40,32... | collective-permute-start | bytes 4718600 | tf_op jit(solution)/shard_map/ppermute | solution.py:12
Sparse Core Ops, SparseCore 0:
  9.5 76.4 all-gather.1
  174.4 52.9 reduce-scatter.1
where the time goes:
time: 235 us; the launch traced here: 234 us
  waiting for transfers between devices  100 us (43%)
  local copies, waits for them, and re-layouts  66.4 us (28%)
  matrix products  19.4 us (8%)
  loops' own time  15.9 us (7%)
  starting transfers between devices  15 us (6%)
  between operations  13.5 us (6%)
  other arithmetic  4.07 us (2%)
    reduce_scatter x1, waiting for transfers between devices, on_device(): lax.psum_scatter(lax.map(one_row, jnp.arange(row_count * lax.axis_size('r...  53.1 us
    gather x16, local copies, waits for them, and re-layouts, one_row(): picked = window_rows[window_idx[row_index][:, None], slot_index[row_index]]  34.9 us
    ppermute x4, waiting for transfers between devices, passed_along(): return lax.ppermute(x, axis, pairs)  31.6 us
    dot_general x8, matrix products, one_row(): jnp.einsum('sab,sfbc->fac', entries[row_index], picked, precision=HIGHEST)  19.4 us
    another operation x1, loops' own time, on_device(): lax.map(one_row, jnp.arange(row_count * lax.axis_size('rep'), dtype=jnp.i...  15.9 us
    ppermute x4, starting transfers between devices, passed_along(): return lax.ppermute(x, axis, pairs)  15 us
    all_gather x1, waiting for transfers between devices, on_device(): gathered = lax.all_gather(p_values, 'rep', axis=1, tiled=True)  14.5 us
    unnamed x7, local copies, waits for them, and re-layouts  11.3 us
  transfers between devices with their start and end apart: 6, of which 4 were waited for; matrix products, arithmetic and copies ran while one was open for 7% of the time, Pallas kernels for 0%

commit v1 on v0

--- a/solution.py
+++ b/solution.py
@@ -1,9 +1,40 @@
+import functools
 import jax
 import jax.numpy as jnp
 from jax import lax
 from jax.sharding import PartitionSpec as P
 
 HIGHEST = lax.Precision.HIGHEST
+
+
+def define_spans(original, link_axis):
+    state_next = lax.axis_size(link_axis)
+    odd = lax.axis_index(link_axis)
+    n_now, w_next, v1 = (state_next, odd, original.shape[1])
+    crops = []
+    for ii, tick in enumerate(original.shape):
+        crops.append(tick * n_now if ii == 1 else tick)
+    high = jnp.zeros(crops, original.dtype)
+    s_next = lax.dynamic_update_slice_in_dim(high, original, w_next * v1, axis=1)
+    newest = main = original
+    for h in range(1, n_now // 2 + 1):
+        items = []
+        for ii in range(n_now):
+            items.append((ii, (ii + 1) % n_now))
+        newest = lax.ppermute(newest, link_axis, items)
+        s_next = lax.dynamic_update_slice_in_dim(s_next, newest, (w_next - h) % n_now * v1, axis=1)
+        if 2 * h < n_now:
+            sheets = []
+            for ii in range(n_now):
+                sheets.append((ii, (ii - 1) % n_now))
+            main = lax.ppermute(main, link_axis, sheets)
+            s_next = lax.dynamic_update_slice_in_dim(
+                s_next, main, (w_next + h) % n_now * v1, axis=1
+            )
+    return s_next
+
+
+compute_the_points = functools.partial(define_spans, link_axis="rep")
 
 
 def passed_along(x, axis, by):
@@ -22,7 +53,7 @@
     block_size = own_rows.shape[2]
     per_layer = slot_total // layers
     seg_rows = row_count * layers
-    gathered = lax.all_gather(p_values, "rep", axis=1, tiled=True)
+    gathered = compute_the_points(p_values)
     entries = lax.dynamic_slice_in_dim(gathered, layer_index * per_layer, per_layer, 2)
     entries = entries.reshape(seg_rows, per_layer, block_size, block_size)
     received = []

time: 235 us -> 243 us (1.034)
  starting transfers between devices: 15 us -> 27.9 us
  waiting for transfers between devices: 100 us -> 95.6 us
    ppermute x0 -> x3, waiting for transfers between devices: none -> 33.4 us  [the longest x2 20.9 us: define_spans(): newest = lax.ppermute(newest, link_axis, items)]
    ppermute x4, waiting for transfers between devices: 31.6 us -> 5.63 us  [passed_along(): return lax.ppermute(x, axis, pairs)]
    ppermute x0 -> x3, starting transfers between devices: none -> 15 us  [the longest x1 8.97 us: define_spans(): main = lax.ppermute(main, link_axis, sheets)]
    all_gather x1 -> x0, waiting for transfers between devices: 14.5 us -> none  [on_device(): gathered = lax.all_gather(p_values, 'rep', axis=1, tiled=True)]
    dynamic_update_slice x0 -> x4, local copies, waits for them, and re-layouts: none -> 4.82 us  [the longest x2 3.07 us: define_spans(): lax.dynamic_update_slice_in_dim(s_next, newest, (w_next - h) % n_now * v1...]
    unnamed x7 -> x9, local copies, waits for them, and re-layouts: 11.3 us -> 6.54 us
    reduce_scatter x1, waiting for transfers between devices: 53.1 us -> 56.6 us  [on_device(): lax.psum_scatter(lax.map(one_row, jnp.arange(row_count * lax.axis_size('r...]
  transfers between devices with their start and end apart: 6 -> 8, of which waited for: 4 -> 5; matrix products, arithmetic and copies ran while one was open for 7% -> 6% of each run, Pallas kernels for 0% -> 0%
where the time goes in v1:
time: 243 us; the launch traced here: 241 us
  waiting for transfers between devices  95.6 us (39%)
  local copies, waits for them, and re-layouts  64.9 us (27%)
  starting transfers between devices  27.9 us (11%)
  matrix products  19.4 us (8%)
  loops' own time  15.9 us (7%)
  between operations  13.6 us (6%)
  other arithmetic  4.08 us (2%)
    reduce_scatter x1, waiting for transfers between devices, on_device(): lax.psum_scatter(lax.map(one_row, jnp.arange(row_count * lax.axis_size('r...  56.6 us
    gather x16, local copies, waits for them, and re-layouts, one_row(): picked = window_rows[window_idx[row_index][:, None], slot_index[row_index]]  34.9 us
    ppermute x2, waiting for transfers between devices, define_spans(): newest = lax.ppermute(newest, link_axis, items)  20.9 us
    dot_general x8, matrix products, one_row(): jnp.einsum('sab,sfbc->fac', entries[row_index], picked, precision=HIGHEST)  19.4 us
    another operation x1, loops' own time, on_device(): lax.map(one_row, jnp.arange(row_count * lax.axis_size('rep'), dtype=jnp.i...  15.9 us
    ppermute x4, starting transfers between devices, passed_along(): return lax.ppermute(x, axis, pairs)  13 us
    ppermute x1, waiting for transfers between devices, define_spans(): main = lax.ppermute(main, link_axis, sheets)  12.4 us
    ppermute x1, starting transfers between devices, define_spans(): main = lax.ppermute(main, link_axis, sheets)  8.97 us
  transfers between devices with their start and end apart: 8, of which 5 were waited for; matrix products, arithmetic and copies ran while one was open for 6% of the time, Pallas kernels for 0%

profile of v1, /device:TPU:1, one launch (start us, length us, event | category | flops | bytes accessed | tf_op | source)
XLA Modules:
  0.0 241.5 jit_solution(14637616190718226669)
XLA Ops:
  6.5 4.1 %collective-permute-start.4 = (f32[2,1,12,128,128]{4,3,2,1,0:T(8,128)}, f32[2,1,12,128,128]{4,3,2,1,0:T(8,128)}, u32[]{:S(2)}, u32[]{:S(2)}) collective-permute-start(f32[2,1,12,128,128]{4,3,2,1,0:T(8,128)} %param.5), channel_id=1, source_target_pairs={{0,1},{1,2},{2,3},{3,0},{4,5},{5,6},{6,7},{7,4},{8,9},{9,10},{10,1... | collective-permute-start | bytes 4718600 | tf_op jit(solution)/shard_map/ppermute | solution.py:24
  10.6 5.2 %collective-permute-start = (f32[2,12,128,128]{3,2,1,0:T(8,128)}, f32[2,12,128,128]{3,2,1,0:T(8,128)}, u32[]{:S(2)}, u32[]{:S(2)}) collective-permute-start(f32[2,12,128,128]{3,2,1,0:T(8,128)} %bitcast.41), channel_id=1, source_target_pairs={{0,8},{4,12},{8,16},{12,20},{16,24},{20,28},{24,32},{28,36},{32,40... | collective-permute-start | bytes 4718600 | tf_op jit(solution)/shard_map/ppermute | solution.py:43
  15.8 4.0 %collective-permute-start.1 = (f32[2,12,128,128]{3,2,1,0:T(8,128)}, f32[2,12,128,128]{3,2,1,0:T(8,128)}, u32[]{:S(2)}, u32[]{:S(2)}) collective-permute-start(f32[2,12,128,128]{3,2,1,0:T(8,128)} %bitcast.42), channel_id=1, source_target_pairs={{0,4},{4,8},{8,12},{12,16},{16,20},{20,24},{24,28},{28,32},{32,36}... | collective-permute-start | bytes 4718600 | tf_op jit(solution)/shard_map/ppermute | solution.py:43
  19.8 2.5 %collective-permute-start.2 = (f32[2,12,128,128]{3,2,1,0:T(8,128)}, f32[2,12,128,128]{3,2,1,0:T(8,128)}, u32[]{:S(2)}, u32[]{:S(2)}) collective-permute-start(f32[2,12,128,128]{3,2,1,0:T(8,128)} %bitcast.43), channel_id=1, source_target_pairs={{4,0},{8,4},{12,8},{16,12},{20,16},{24,20},{28,24},{32,28},{36,32}... | collective-permute-start | bytes 4718600 | tf_op jit(solution)/shard_map/ppermute | solution.py:43
  23.6 1.9 copy.17
  25.5 14.9 %collective-permute-done.4 = f32[2,1,12,128,128]{4,3,2,1,0:T(8,128)} collective-permute-done((f32[2,1,12,128,128]{4,3,2,1,0:T(8,128)}, f32[2,1,12,128,128]{4,3,2,1,0:T(8,128)}, u32[]{:S(2)}, u32[]{:S(2)}) %collective-permute-start.4) | collective-permute-done | bytes 1572896 | tf_op jit(solution)/shard_map/ppermute | solution.py:24
  40.4 9.0 %collective-permute-start.5 = (f32[2,1,12,128,128]{4,3,2,1,0:T(8,128)}, f32[2,1,12,128,128]{4,3,2,1,0:T(8,128)}, u32[]{:S(2)}, u32[]{:S(2)}) collective-permute-start(f32[2,1,12,128,128]{4,3,2,1,0:T(8,128)} %param.5), channel_id=1, source_target_pairs={{0,3},{1,0},{2,1},{3,2},{4,7},{5,4},{6,5},{7,6},{8,11},{9,8},{10,9... | collective-permute-start | bytes 4718600 | tf_op jit(solution)/shard_map/ppermute | solution.py:30
  50.2 1.6 gather_fusion.1
  51.9 1.9 collective-permute-start.6
  58.8 1.5 constant_dynamic-update-slice_fusion.8
  60.4 5.6 %collective-permute-done.1 = f32[2,12,128,128]{3,2,1,0:T(8,128)} collective-permute-done((f32[2,12,128,128]{3,2,1,0:T(8,128)}, f32[2,12,128,128]{3,2,1,0:T(8,128)}, u32[]{:S(2)}, u32[]{:S(2)}) %collective-permute-start.1) | collective-permute-done | bytes 1572896 | tf_op jit(solution)/shard_map/ppermute | solution.py:43
  69.3 12.4 %collective-permute-done.5 = f32[2,1,12,128,128]{4,3,2,1,0:T(8,128)} collective-permute-done((f32[2,1,12,128,128]{4,3,2,1,0:T(8,128)}, f32[2,1,12,128,128]{4,3,2,1,0:T(8,128)}, u32[]{:S(2)}, u32[]{:S(2)}) %collective-permute-start.5) | collective-permute-done | bytes 1572896 | tf_op jit(solution)/shard_map/ppermute | solution.py:30
  83.3 6.0 %collective-permute-done.6 = f32[2,1,12,128,128]{4,3,2,1,0:T(8,128)} collective-permute-done((f32[2,1,12,128,128]{4,3,2,1,0:T(8,128)}, f32[2,1,12,128,128]{4,3,2,1,0:T(8,128)}, u32[]{:S(2)}, u32[]{:S(2)}) %collective-permute-start.6) | collective-permute-done | bytes 1572896 | tf_op jit(solution)/shard_map/ppermute | solution.py:24
  89.3 1.5 constant_dynamic-update-slice_fusion.6
  92.2 85.7 %while.10 = (s32[]{:T(128)}, f32[8,8,128,128]{3,2,1,0:T(8,128)}, s32[8]{0:T(128)S(1)}, pred[8,3,8]{2,1,0:T(4,128)(4,1)S(1)}, s32[8,3]{1,0:T(8,128)S(1)}, /*index...) while((s32[]{:T(128)}, f32[8,8,128,128]{3,2,1,0:T(8,128)}, ...), condition=%wide.region_3.4_spmd, body=%wide.region_2.3_spmd.sunk | while | flops 604373184 | bytes 10683783 | solution.py:81
  95.0 3.9 %gather_fusion = f32[24,128,128]{2,1,0:T(8,128)S(1)} fusion(f32[10,12,128,128]{3,2,1,0:T(8,128)} %get-tuple-element.151, s32[24]{0:T(128)S(1)} %reshape.83), kind=kCustom, calls=%fused_computation.clone.1 | custom fusion | bytes 3145920 | tf_op jit(solution)/shard_map/while/body/eval_jaxpr/gather | solution.py:76
  99.4 2.4 %fusion.27 = f32[1,8,128,128]{2,3,1,0:T(8,128)S(1)} fusion(f32[3,8,128,128]{2,3,0,1:T(8,128)S(1)} %copy.26, pred[3,8]{0,1:T(8,128)(4,1)S(1)} %copy.27, f32[8,3,128,128]{3,2,1,0:T(8,128)} %get-tuple-element.152, s32[]{:T(128)S(6)} %select_n.116), kind=kOutput, calls=%fused_computation.4.clone.1 | convolution fusion | flops 604372992 | bytes 2293788 | tf_op jit(solution)/shard_map/while/body/eval_jaxpr/sab,sfbc->fac/dot_general | solution.py:78
  105.7 3.9 %gather_fusion = f32[24,128,128]{2,1,0:T(8,128)S(1)} fusion(f32[10,12,128,128]{3,2,1,0:T(8,128)} %get-tuple-element.151, s32[24]{0:T(128)S(1)} %reshape.83), kind=kCustom, calls=%fused_computation.clone.1 | custom fusion | bytes 3145920 | tf_op jit(solution)/shard_map/while/body/eval_jaxpr/gather | solution.py:76
  110.2 2.4 %fusion.27 = f32[1,8,128,128]{2,3,1,0:T(8,128)S(1)} fusion(f32[3,8,128,128]{2,3,0,1:T(8,128)S(1)} %copy.26, pred[3,8]{0,1:T(8,128)(4,1)S(1)} %copy.27, f32[8,3,128,128]{3,2,1,0:T(8,128)} %get-tuple-element.152, s32[]{:T(128)S(6)} %select_n.116), kind=kOutput, calls=%fused_computation.4.clone.1 | convolution fusion | flops 604372992 | bytes 2293788 | tf_op jit(solution)/shard_map/while/body/eval_jaxpr/sab,sfbc->fac/dot_general | solution.py:78
  116.4 3.9 %gather_fusion = f32[24,128,128]{2,1,0:T(8,128)S(1)} fusion(f32[10,12,128,128]{3,2,1,0:T(8,128)} %get-tuple-element.151, s32[24]{0:T(128)S(1)} %reshape.83), kind=kCustom, calls=%fused_computation.clone.1 | custom fusion | bytes 3145920 | tf_op jit(solution)/shard_map/while/body/eval_jaxpr/gather | solution.py:76
  120.9 2.4 %fusion.27 = f32[1,8,128,128]{2,3,1,0:T(8,128)S(1)} fusion(f32[3,8,128,128]{2,3,0,1:T(8,128)S(1)} %copy.26, pred[3,8]{0,1:T(8,128)(4,1)S(1)} %copy.27, f32[8,3,128,128]{3,2,1,0:T(8,128)} %get-tuple-element.152, s32[]{:T(128)S(6)} %select_n.116), kind=kOutput, calls=%fused_computation.4.clone.1 | convolution fusion | flops 604372992 | bytes 2293788 | tf_op jit(solution)/shard_map/while/body/eval_jaxpr/sab,sfbc->fac/dot_general | solution.py:78
  127.2 3.9 %gather_fusion = f32[24,128,128]{2,1,0:T(8,128)S(1)} fusion(f32[10,12,128,128]{3,2,1,0:T(8,128)} %get-tuple-element.151, s32[24]{0:T(128)S(1)} %reshape.83), kind=kCustom, calls=%fused_computation.clone.1 | custom fusion | bytes 3145920 | tf_op jit(solution)/shard_map/while/body/eval_jaxpr/gather | solution.py:76
  131.7 2.4 %fusion.27 = f32[1,8,128,128]{2,3,1,0:T(8,128)S(1)} fusion(f32[3,8,128,128]{2,3,0,1:T(8,128)S(1)} %copy.26, pred[3,8]{0,1:T(8,128)(4,1)S(1)} %copy.27, f32[8,3,128,128]{3,2,1,0:T(8,128)} %get-tuple-element.152, s32[]{:T(128)S(6)} %select_n.116), kind=kOutput, calls=%fused_computation.4.clone.1 | convolution fusion | flops 604372992 | bytes 2293788 | tf_op jit(solution)/shard_map/while/body/eval_jaxpr/sab,sfbc->fac/dot_general | solution.py:78
  137.9 3.9 %gather_fusion = f32[24,128,128]{2,1,0:T(8,128)S(1)} fusion(f32[10,12,128,128]{3,2,1,0:T(8,128)} %get-tuple-element.151, s32[24]{0:T(128)S(1)} %reshape.83), kind=kCustom, calls=%fused_computation.clone.1 | custom fusion | bytes 3145920 | tf_op jit(solution)/shard_map/while/body/eval_jaxpr/gather | solution.py:76
  142.4 2.4 %fusion.27 = f32[1,8,128,128]{2,3,1,0:T(8,128)S(1)} fusion(f32[3,8,128,128]{2,3,0,1:T(8,128)S(1)} %copy.26, pred[3,8]{0,1:T(8,128)(4,1)S(1)} %copy.27, f32[8,3,128,128]{3,2,1,0:T(8,128)} %get-tuple-element.152, s32[]{:T(128)S(6)} %select_n.116), kind=kOutput, calls=%fused_computation.4.clone.1 | convolution fusion | flops 604372992 | bytes 2293788 | tf_op jit(solution)/shard_map/while/body/eval_jaxpr/sab,sfbc->fac/dot_general | solution.py:78
  148.6 3.9 %gather_fusion = f32[24,128,128]{2,1,0:T(8,128)S(1)} fusion(f32[10,12,128,128]{3,2,1,0:T(8,128)} %get-tuple-element.151, s32[24]{0:T(128)S(1)} %reshape.83), kind=kCustom, calls=%fused_computation.clone.1 | custom fusion | bytes 3145920 | tf_op jit(solution)/shard_map/while/body/eval_jaxpr/gather | solution.py:76
  153.1 2.4 %fusion.27 = f32[1,8,128,128]{2,3,1,0:T(8,128)S(1)} fusion(f32[3,8,128,128]{2,3,0,1:T(8,128)S(1)} %copy.26, pred[3,8]{0,1:T(8,128)(4,1)S(1)} %copy.27, f32[8,3,128,128]{3,2,1,0:T(8,128)} %get-tuple-element.152, s32[]{:T(128)S(6)} %select_n.116), kind=kOutput, calls=%fused_computation.4.clone.1 | convolution fusion | flops 604372992 | bytes 2293788 | tf_op jit(solution)/shard_map/while/body/eval_jaxpr/sab,sfbc->fac/dot_general | solution.py:78
  159.3 3.9 %gather_fusion = f32[24,128,128]{2,1,0:T(8,128)S(1)} fusion(f32[10,12,128,128]{3,2,1,0:T(8,128)} %get-tuple-element.151, s32[24]{0:T(128)S(1)} %reshape.83), kind=kCustom, calls=%fused_computation.clone.1 | custom fusion | bytes 3145920 | tf_op jit(solution)/shard_map/while/body/eval_jaxpr/gather | solution.py:76
  163.8 2.4 %fusion.27 = f32[1,8,128,128]{2,3,1,0:T(8,128)S(1)} fusion(f32[3,8,128,128]{2,3,0,1:T(8,128)S(1)} %copy.26, pred[3,8]{0,1:T(8,128)(4,1)S(1)} %copy.27, f32[8,3,128,128]{3,2,1,0:T(8,128)} %get-tuple-element.152, s32[]{:T(128)S(6)} %select_n.116), kind=kOutput, calls=%fused_computation.4.clone.1 | convolution fusion | flops 604372992 | bytes 2293788 | tf_op jit(solution)/shard_map/while/body/eval_jaxpr/sab,sfbc->fac/dot_general | solution.py:78
  170.0 3.9 %gather_fusion = f32[24,128,128]{2,1,0:T(8,128)S(1)} fusion(f32[10,12,128,128]{3,2,1,0:T(8,128)} %get-tuple-element.151, s32[24]{0:T(128)S(1)} %reshape.83), kind=kCustom, calls=%fused_computation.clone.1 | custom fusion | bytes 3145920 | tf_op jit(solution)/shard_map/while/body/eval_jaxpr/gather | solution.py:76
  174.5 2.4 %fusion.27 = f32[1,8,128,128]{2,3,1,0:T(8,128)S(1)} fusion(f32[3,8,128,128]{2,3,0,1:T(8,128)S(1)} %copy.26, pred[3,8]{0,1:T(8,128)(4,1)S(1)} %copy.27, f32[8,3,128,128]{3,2,1,0:T(8,128)} %get-tuple-element.152, s32[]{:T(128)S(6)} %select_n.116), kind=kOutput, calls=%fused_computation.4.clone.1 | convolution fusion | flops 604372992 | bytes 2293788 | tf_op jit(solution)/shard_map/while/body/eval_jaxpr/sab,sfbc->fac/dot_general | solution.py:78
  178.0 56.6 %reduce-scatter.2.cloned.1.call-done = f32[2,8,128,128]{3,2,1,0:T(8,128)} async-done(((f32[8,8,128,128]{3,2,1,0:T(8,128)}), f32[2,8,128,128]{3,2,1,0:T(8,128)}) %reduce-scatter.2.cloned.1.call-update) | async-done | bytes 1048592 | tf_op jit(solution)/shard_map/reduce_scatter | solution.py:80
  (100 shorter events, 32.5 us)
Async XLA Ops:
  6.5 50.5 %copy-start.1 = (f32[2,1,12,128,128]{4,3,2,1,0:T(8,128)S(1)}, f32[2,1,12,128,128]{4,3,2,1,0:T(8,128)}, u32[]{:S(2)}) copy-start(f32[2,1,12,128,128]{4,3,2,1,0:T(8,128)} %param.5) | copy-start | bytes 4718596
  6.5 228.1 %reduce-scatter.2.cloned.1.call-start = ((), (), s32[]{:S(2)}) async-start(), calls=%async_computation.1 | async-start | bytes 5242880 | tf_op jit(solution)/shard_map/reduce_scatter | solution.py:80
  6.5 33.8 %collective-permute-start.4 = (f32[2,1,12,128,128]{4,3,2,1,0:T(8,128)}, f32[2,1,12,128,128]{4,3,2,1,0:T(8,128)}, u32[]{:S(2)}, u32[]{:S(2)}) collective-permute-start(f32[2,1,12,128,128]{4,3,2,1,0:T(8,128)} %param.5), channel_id=1, source_target_pairs={{0,1},{1,2},{2,3},{3,0},{4,5},{5,6},{6,7},{7,4},{8,9},{9,10},{10,1... | collective-permute-start | bytes 4718600 | tf_op jit(solution)/shard_map/ppermute | solution.py:24
  10.6 41.2 %collective-permute-start = (f32[2,12,128,128]{3,2,1,0:T(8,128)}, f32[2,12,128,128]{3,2,1,0:T(8,128)}, u32[]{:S(2)}, u32[]{:S(2)}) collective-permute-start(f32[2,12,128,128]{3,2,1,0:T(8,128)} %bitcast.41), channel_id=1, source_target_pairs={{0,8},{4,12},{8,16},{12,20},{16,24},{20,28},{24,32},{28,36},{32,40... | collective-permute-start | bytes 4718600 | tf_op jit(solution)/shard_map/ppermute | solution.py:43
  15.8 50.2 %collective-permute-start.1 = (f32[2,12,128,128]{3,2,1,0:T(8,128)}, f32[2,12,128,128]{3,2,1,0:T(8,128)}, u32[]{:S(2)}, u32[]{:S(2)}) collective-permute-start(f32[2,12,128,128]{3,2,1,0:T(8,128)} %bitcast.42), channel_id=1, source_target_pairs={{0,4},{4,8},{8,12},{12,16},{16,20},{20,24},{24,28},{28,32},{32,36}... | collective-permute-start | bytes 4718600 | tf_op jit(solution)/shard_map/ppermute | solution.py:43
  19.8 47.9 %collective-permute-start.2 = (f32[2,12,128,128]{3,2,1,0:T(8,128)}, f32[2,12,128,128]{3,2,1,0:T(8,128)}, u32[]{:S(2)}, u32[]{:S(2)}) collective-permute-start(f32[2,12,128,128]{3,2,1,0:T(8,128)} %bitcast.43), channel_id=1, source_target_pairs={{4,0},{8,4},{12,8},{16,12},{20,16},{24,20},{28,24},{32,28},{36,32}... | collective-permute-start | bytes 4718600 | tf_op jit(solution)/shard_map/ppermute | solution.py:43
  22.3 46.9 %collective-permute-start.3 = (f32[2,12,128,128]{3,2,1,0:T(8,128)}, f32[2,12,128,128]{3,2,1,0:T(8,128)S(1)}, u32[]{:S(2)}, u32[]{:S(2)}) collective-permute-start(f32[2,12,128,128]{3,2,1,0:T(8,128)} %bitcast.44), channel_id=1, source_target_pairs={{8,0},{12,4},{16,8},{20,12},{24,16},{28,20},{32,24},{36,28},{40,32... | collective-permute-start | bytes 4718600 | tf_op jit(solution)/shard_map/ppermute | solution.py:43
  40.4 41.4 %collective-permute-start.5 = (f32[2,1,12,128,128]{4,3,2,1,0:T(8,128)}, f32[2,1,12,128,128]{4,3,2,1,0:T(8,128)}, u32[]{:S(2)}, u32[]{:S(2)}) collective-permute-start(f32[2,1,12,128,128]{4,3,2,1,0:T(8,128)} %param.5), channel_id=1, source_target_pairs={{0,3},{1,0},{2,1},{3,2},{4,7},{5,4},{6,5},{7,6},{8,11},{9,8},{10,9... | collective-permute-start | bytes 4718600 | tf_op jit(solution)/shard_map/ppermute | solution.py:30
  51.9 37.5 %collective-permute-start.6 = (f32[2,1,12,128,128]{4,3,2,1,0:T(8,128)}, f32[2,1,12,128,128]{4,3,2,1,0:T(8,128)}, u32[]{:S(2)}, u32[]{:S(2)}) collective-permute-start(f32[2,1,12,128,128]{4,3,2,1,0:T(8,128)} %collective-permute-done.4), channel_id=1, source_target_pairs={{0,1},{1,2},{2,3},{3,0},{4,5},{5,6},{6,7},{7,4},{8,9},{9,10},{10,1... | collective-permute-start | bytes 4718600 | tf_op jit(solution)/shard_map/ppermute | solution.py:24
  69.3 22.9 %copy-start = (f32[10,12,128,128]{3,2,1,0:T(8,128)}, f32[10,12,128,128]{3,2,1,0:T(8,128)S(1)}, u32[]{:S(2)}) copy-start(f32[10,12,128,128]{3,2,1,0:T(8,128)S(1)} %constant_dynamic-update-slice_fusion.1) | copy-start | bytes 23592964
Sparse Core Ops, SparseCore 0:
  178.1 56.4 reduce-scatter.1
